TPU v7x, 512 devices: a whole 4x4x16 slice. The times are simulated.
512 devices in a mesh: grp: 64 (over z, x_lo, core), rep: 8 (over y, x_hi).
Axes of the slice: x: 4 (x_hi: 2, x_lo: 2; x = x_hi * 2 + x_lo), y: 4, z: 16, core: 2. Of those that a mesh axis runs over, the one named last changes fastest.
Arguments:
- adjoint: bfloat16 [1024, 512], P('grp'), may hold values from -6 to 6
- active: int32 [1024, 512], P('grp'), may hold values 0 or 1
- counts: int32 [1024, 65536], P('rep', 'grp'), may hold values from 0 to 3, as said below
- src_degree: int32 [1024], P('rep'), may hold values from 8 to 256
- dst_degree: int32 [65536], P('grp'), may hold values from 8 to 256
- inputs: bfloat16 [65536, 512], P(('grp', 'rep')), may hold values from -6 to 6
- weight: bfloat16 [512, 512], replicated, may hold values from -0.25 to 0.25
Outputs:
- grad_input: bfloat16 [65536, 512], P(('grp', 'rep'))
- grad_weight: float32 [512, 512], P('rep')
Inputs may be any that keep to these rules, and one draw needn't show every extreme that they name: Edge counts; within an aligned tile of 16 source rows by 1024 destination columns the share of nonzero entries ranges from none to all, differing from tile to tile.
All inputs are finite; a program needn't handle non-finite values. No bound on the sum of `active` on one device may be relied on, other than what follows from the above.
Results may differ from a plain program's by a relative error of at most 0.0057.
Values may be sent and summed in bfloat16 or wider, within the bound.
A program may use at most 64 MiB of HBM per device.

v0:
```python
import jax
import jax.numpy as jnp
from jax import lax
from jax.sharding import PartitionSpec as P


def spread(shard, axis, root):
    mine = lax.axis_index(axis) == root
    return lax.psum(jnp.where(mine, shard, jnp.zeros_like(shard)), axis)


def weight_term(row_inputs, values):
    high_part = values.astype(jnp.bfloat16)
    low_part = (values - high_part.astype(jnp.float32)).astype(jnp.bfloat16)
    upper = lax.dot_general(
        row_inputs, high_part, (((0,), (0,)), ((), ())), preferred_element_type=jnp.float32
    )
    lower = lax.dot_general(
        row_inputs, low_part, (((0,), (0,)), ((), ())), preferred_element_type=jnp.float32
    )
    return upper + lower


def body(adjoint, active, counts, src_degree, dst_degree, inputs, weight):
    masked = (adjoint.astype(jnp.float32) * active.astype(jnp.float32)).astype(jnp.bfloat16)
    src_scale = lax.rsqrt(src_degree.astype(jnp.float32))
    dst_scale = lax.rsqrt(dst_degree.astype(jnp.float32))
    src_rows = adjoint.shape[0]
    blocks = counts.shape[0] // src_rows
    replica = lax.axis_index("rep")

    def scaled_product(count_tile, row_scale, owner_rows, running):
        scaled_tile = (
            count_tile.astype(jnp.float32) * row_scale[:, None] * dst_scale[None, :]
        ).astype(jnp.bfloat16)
        return running + lax.dot_general(
            scaled_tile, owner_rows, (((0,), (0,)), ((), ())), preferred_element_type=jnp.float32
        )

    def apply_tile(block_index, running):
        owner_index = replica * blocks + block_index
        owner_rows = spread(masked, "grp", owner_index)
        start = block_index * src_rows
        count_tile = lax.dynamic_slice_in_dim(counts, start, src_rows, 0)
        row_scale = lax.dynamic_slice_in_dim(src_scale, start, src_rows, 0)
        return scaled_product(count_tile, row_scale, owner_rows, running)

    partial_value = lax.fori_loop(
        0, blocks, apply_tile, jnp.zeros((counts.shape[1], masked.shape[1]), jnp.float32)
    )
    grad_pre = lax.psum_scatter(partial_value, "rep", scatter_dimension=0, tiled=True)
    grad_input = lax.dot_general(
        grad_pre.astype(jnp.bfloat16),
        weight,
        (((1,), (1,)), ((), ())),
        preferred_element_type=jnp.float32,
    ).astype(jnp.bfloat16)
    vertex_total = inputs.shape[0] * lax.axis_size("grp") * lax.axis_size("rep")
    local_term = weight_term(inputs, grad_pre)
    whole_term = lax.psum(local_term, "grp")
    grad_weight = lax.psum_scatter(whole_term, "rep", scatter_dimension=0, tiled=True)
    return (grad_input, grad_weight / vertex_total)


def solution(mesh):
    in_specs = (
        P("grp", None),
        P("grp", None),
        P("rep", "grp"),
        P("rep"),
        P("grp"),
        P(("grp", "rep"), None),
        P(),
    )
    out_specs = (P(("grp", "rep"), None), P("rep", None))
    return jax.shard_map(body, mesh=mesh, in_specs=in_specs, out_specs=out_specs, check_vma=False)
```

profile of v0, /device:TPU:1, one launch (start us, length us, event | category | flops | bytes accessed | tf_op | source)
XLA Modules:
  0.0 2293.0 jit_solution(14087357009032355527)
XLA Ops:
  7.2 0.0 copy-start
  7.2 0.0 reduce-scatter.5.cloned.1.call-start
  7.2 0.7 convert_rsqrt_fusion.1
  7.9 0.7 convert_rsqrt_fusion
  8.6 0.8 multiply_convert_fusion.2
  9.4 1680.2 %while.16 = (s32[]{:T(128)}, f32[1024,512]{1,0:T(8,128)S(1)}, s32[128,1024]{1,0:T(8,128)}, f32[128]{0:T(128)S(1)}, f32[1024]{0:T(1024)S(1)}, /*index=5*/s32[]{:T...) while((s32[]{:T(128)}, f32[1024,512]{1,0:T(8,128)S(1)}, ...), condition=%wide.region_2.3_spmd.clone, body=%wide.region_0.2_spmd.clone.sunk | while | flops 17907724 | bytes 4346299 | solution.py:48
  9.4 0.1 dynamic_slice.25
  9.5 214.4 %psum.24 = bf16[16,512]{1,0:T(8,128)(2,1)S(1)} all-reduce(bf16[16,512]{1,0:T(8,128)(2,1)S(1)} %broadcast_select_fusion.2), channel_id=1, replica_groups=mesh['grp'=64,'rep'=8] {'grp'}, use_global_device_ids=true, to_apply=%region_1.1 | all-reduce | flops 8192 | bytes 32768 | tf_op jit(solution)/shard_map/while/body/eval_jaxpr/psum | solution.py:9
  223.9 1.6 select_add_fusion.2
  225.5 0.1 dynamic_slice.25
  225.6 207.5 %psum.24 = bf16[16,512]{1,0:T(8,128)(2,1)S(1)} all-reduce(bf16[16,512]{1,0:T(8,128)(2,1)S(1)} %broadcast_select_fusion.2), channel_id=1, replica_groups=mesh['grp'=64,'rep'=8] {'grp'}, use_global_device_ids=true, to_apply=%region_1.1 | all-reduce | flops 8192 | bytes 32768 | tf_op jit(solution)/shard_map/while/body/eval_jaxpr/psum | solution.py:9
  433.1 1.5 select_add_fusion.2
  434.6 0.1 dynamic_slice.25
  434.7 207.5 %psum.24 = bf16[16,512]{1,0:T(8,128)(2,1)S(1)} all-reduce(bf16[16,512]{1,0:T(8,128)(2,1)S(1)} %broadcast_select_fusion.2), channel_id=1, replica_groups=mesh['grp'=64,'rep'=8] {'grp'}, use_global_device_ids=true, to_apply=%region_1.1 | all-reduce | flops 8192 | bytes 32768 | tf_op jit(solution)/shard_map/while/body/eval_jaxpr/psum | solution.py:9
  642.2 1.6 select_add_fusion.2
  643.8 0.1 dynamic_slice.25
  643.9 207.5 %psum.24 = bf16[16,512]{1,0:T(8,128)(2,1)S(1)} all-reduce(bf16[16,512]{1,0:T(8,128)(2,1)S(1)} %broadcast_select_fusion.2), channel_id=1, replica_groups=mesh['grp'=64,'rep'=8] {'grp'}, use_global_device_ids=true, to_apply=%region_1.1 | all-reduce | flops 8192 | bytes 32768 | tf_op jit(solution)/shard_map/while/body/eval_jaxpr/psum | solution.py:9
  851.4 1.5 select_add_fusion.2
  853.0 0.1 dynamic_slice.25
  853.1 207.5 %psum.24 = bf16[16,512]{1,0:T(8,128)(2,1)S(1)} all-reduce(bf16[16,512]{1,0:T(8,128)(2,1)S(1)} %broadcast_select_fusion.2), channel_id=1, replica_groups=mesh['grp'=64,'rep'=8] {'grp'}, use_global_device_ids=true, to_apply=%region_1.1 | all-reduce | flops 8192 | bytes 32768 | tf_op jit(solution)/shard_map/while/body/eval_jaxpr/psum | solution.py:9
  1060.6 1.6 select_add_fusion.2
  1062.2 0.1 dynamic_slice.25
  1062.2 207.5 %psum.24 = bf16[16,512]{1,0:T(8,128)(2,1)S(1)} all-reduce(bf16[16,512]{1,0:T(8,128)(2,1)S(1)} %broadcast_select_fusion.2), channel_id=1, replica_groups=mesh['grp'=64,'rep'=8] {'grp'}, use_global_device_ids=true, to_apply=%region_1.1 | all-reduce | flops 8192 | bytes 32768 | tf_op jit(solution)/shard_map/while/body/eval_jaxpr/psum | solution.py:9
  1269.7 1.5 select_add_fusion.2
  1271.3 0.1 dynamic_slice.25
  1271.4 207.5 %psum.24 = bf16[16,512]{1,0:T(8,128)(2,1)S(1)} all-reduce(bf16[16,512]{1,0:T(8,128)(2,1)S(1)} %broadcast_select_fusion.2), channel_id=1, replica_groups=mesh['grp'=64,'rep'=8] {'grp'}, use_global_device_ids=true, to_apply=%region_1.1 | all-reduce | flops 8192 | bytes 32768 | tf_op jit(solution)/shard_map/while/body/eval_jaxpr/psum | solution.py:9
  1478.9 1.6 select_add_fusion.2
  1480.5 0.1 dynamic_slice.25
  1480.6 207.5 %psum.24 = bf16[16,512]{1,0:T(8,128)(2,1)S(1)} all-reduce(bf16[16,512]{1,0:T(8,128)(2,1)S(1)} %broadcast_select_fusion.2), channel_id=1, replica_groups=mesh['grp'=64,'rep'=8] {'grp'}, use_global_device_ids=true, to_apply=%region_1.1 | all-reduce | flops 8192 | bytes 32768 | tf_op jit(solution)/shard_map/while/body/eval_jaxpr/psum | solution.py:9
  1688.1 1.5 select_add_fusion.2
  1689.6 0.0 copy-start.1
  1689.7 0.0 copy-start.3
  1689.7 1.3 copy-done.1
  1691.0 0.0 reduce-scatter.5.cloned.1.call-update
  1691.0 0.0 reduce-scatter.7.cloned.1.call-start
  1691.1 89.1 %reduce-scatter.5.cloned.1.call-done = f32[128,512]{1,0:T(8,128)} async-done(((f32[1024,512]{1,0:T(8,128)}), f32[128,512]{1,0:T(8,128)}) %reduce-scatter.5.cloned.1.call-update) | async-done | bytes 262160 | tf_op jit(solution)/shard_map/reduce_scatter | solution.py:51
  1780.1 0.0 copy-done.3
  1780.1 1.3 fusion.5
  1781.4 1.4 fusion.3
  1782.7 0.0 copy-start.2
  1782.8 1.3 copy.11
  1784.1 0.0 reduce-scatter.7.cloned.1.call-update
  1784.1 0.0 all-reduce.2.cloned.1.call-start
  1784.1 86.7 %reduce-scatter.7.cloned.1.call-done = f32[64,512]{1,0:T(8,128)} async-done(((f32[512,512]{1,0:T(8,128)}), f32[64,512]{1,0:T(8,128)}) %reduce-scatter.7.cloned.1.call-update) | async-done | bytes 131088
  1870.9 1.7 copy.12
  1872.6 0.0 all-reduce.2.cloned.1.call-update
  1872.6 0.0 copy-done
  1872.6 0.0 copy-done.2
  1872.6 1.0 convolution_convert_fusion
  1873.6 411.2 %all-reduce.2.cloned.1.call-done = f32[64,512]{0,1:T(8,128)} async-done(((f32[64,512]{0,1:T(8,128)}), f32[64,512]{0,1:T(8,128)}) %all-reduce.2.cloned.1.call-update) | async-done | bytes 131088 | tf_op jit(solution)/shard_map/psum | solution.py:60
  2284.8 1.0 broadcast_multiply_fusion
  2285.7 0.8 copy.10
  (9 shorter events, 0.1 us)
Async XLA Ops:
  7.2 1865.5 %copy-start = (bf16[512,512]{1,0:T(8,128)(2,1)S(1)}, bf16[512,512]{1,0:T(8,128)(2,1)}, u32[]{:S(2)}) copy-start(bf16[512,512]{1,0:T(8,128)(2,1)} %param.15) | copy-start | bytes 1572868
  7.2 1772.9 %reduce-scatter.5.cloned.1.call-start = ((), (), s32[]{:S(2)}) async-start(), calls=%async_computation.2 | async-start | bytes 2359296 | tf_op jit(solution)/shard_map/reduce_scatter | solution.py:51
  1689.6 1.3 copy-start.1
  1689.7 90.5 %copy-start.3 = (bf16[128,512]{1,0:T(8,128)(2,1)S(1)}, bf16[128,512]{1,0:T(8,128)(2,1)}, u32[]{:S(2)}) copy-start(bf16[128,512]{1,0:T(8,128)(2,1)} %param.14) | copy-start | bytes 393220
  1691.0 179.9 %reduce-scatter.7.cloned.1.call-start = ((), (), s32[]{:S(2)}) async-start(), calls=%async_computation.4 | async-start | bytes 1179648
  1782.7 89.9 %copy-start.2 = (f32[128,512]{1,0:T(8,128)S(1)}, f32[128,512]{1,0:T(8,128)}, u32[]{:S(2)}) copy-start(f32[128,512]{1,0:T(8,128)} %reduce-scatter.5.cloned.1.call-done) | copy-start | bytes 786436
  1784.1 500.7 %all-reduce.2.cloned.1.call-start = ((), (), s32[]{:S(2)}) async-start(), calls=%async_computation.3 | async-start | bytes 524288 | tf_op jit(solution)/shard_map/psum | solution.py:60
Sparse Core Ops, SparseCore 0:
  1691.1 88.9 reduce-scatter.4
  1784.6 86.2 reduce-scatter.6
  1873.8 410.9 all-reduce.1
where the time goes:
time: 2290 us
  blocking collectives  1670 us (73%)
  waiting for transfers between devices  587 us (26%)
    psum x8, blocking collectives, spread(): return lax.psum(jnp.where(mine, shard, jnp.zeros_like(shard)), axis)  1670 us
    psum x1, waiting for transfers between devices, body(): whole_term = lax.psum(local_term, 'grp')  411 us
    reduce_scatter x1, waiting for transfers between devices, body(): lax.psum_scatter(partial_value, 'rep', scatter_dimension=0, tiled=True)  89.1 us
    unnamed x4, waiting for transfers between devices  86.8 us
  transfers between devices with their start and end apart: 3, of which 3 were waited for; matrix products, arithmetic and copies ran while one was open for 0% of the time, Pallas kernels for 0%

commit v1 on v0

v1 whole, which is shorter than its diff:
```python
import jax
import jax.numpy as jnp
from jax import lax
from jax.sharding import PartitionSpec as P


def body(adjoint, active, counts, src_degree, dst_degree, inputs, weight):
    masked = (adjoint.astype(jnp.float32) * active.astype(jnp.float32)).astype(jnp.bfloat16)
    src_scale = lax.rsqrt(src_degree.astype(jnp.float32))
    dst_scale = lax.rsqrt(dst_degree.astype(jnp.float32))
    scaled = (counts.astype(jnp.float32) * src_scale[:, None] * dst_scale[None, :]).astype(jnp.bfloat16)
    my_scaled = lax.all_to_all(scaled, "rep", split_axis=1, concat_axis=0, tiled=True)
    all_masked = lax.all_gather(masked, "grp", axis=0, tiled=True)
    grad_pre = lax.dot_general(
        my_scaled, all_masked, (((0,), (0,)), ((), ())), preferred_element_type=jnp.float32
    )
    high = grad_pre.astype(jnp.bfloat16)
    low = (grad_pre - high.astype(jnp.float32)).astype(jnp.bfloat16)
    grad_input = lax.dot_general(
        high, weight, (((1,), (1,)), ((), ())), preferred_element_type=jnp.float32
    ).astype(jnp.bfloat16)
    vertex_total = inputs.shape[0] * lax.axis_size("grp") * lax.axis_size("rep")
    upper = lax.dot_general(inputs, high, (((0,), (0,)), ((), ())), preferred_element_type=jnp.float32)
    lower = lax.dot_general(inputs, low, (((0,), (0,)), ((), ())), preferred_element_type=jnp.float32)
    part = lax.psum_scatter(upper + lower, "rep", scatter_dimension=0, tiled=True)
    grad_weight = lax.psum(part, "grp")
    return (grad_input, grad_weight / vertex_total)


def solution(mesh):
    in_specs = (
        P("grp", None),
        P("grp", None),
        P("rep", "grp"),
        P("rep"),
        P("grp"),
        P(("grp", "rep"), None),
        P(),
    )
    out_specs = (P(("grp", "rep"), None), P("rep", None))
    return jax.shard_map(body, mesh=mesh, in_specs=in_specs, out_specs=out_specs, check_vma=False)
```

time: 2290 us -> 647 us (0.28)
  blocking collectives: 1670 us -> 15.2 us
    psum x8 -> x0, blocking collectives: 1670 us -> none  [spread(): return lax.psum(jnp.where(mine, shard, jnp.zeros_like(shard)), axis)]
    all_gather x0 -> x1, waiting for transfers between devices: none -> 112 us  [body(): all_masked = lax.all_gather(masked, 'grp', axis=0, tiled=True)]
    reduce_scatter x1 -> x0, waiting for transfers between devices: 89.1 us -> none  [body(): lax.psum_scatter(partial_value, 'rep', scatter_dimension=0, tiled=True)]
where the time goes in v1:
time: 647 us
  waiting for transfers between devices  607 us (94%)
  blocking collectives  15.2 us (2%)
  between operations  13.9 us (2%)
    psum x1, waiting for transfers between devices, body(): grad_weight = lax.psum(part, 'grp')  412 us
    all_gather x1, waiting for transfers between devices, body(): all_masked = lax.all_gather(masked, 'grp', axis=0, tiled=True)  112 us
    unnamed x4, waiting for transfers between devices  82.9 us
    all_to_all x1, blocking collectives, body(): lax.all_to_all(scaled, 'rep', split_axis=1, concat_axis=0, tiled=True)  15.2 us
  transfers between devices with their start and end apart: 3, of which 3 were waited for; matrix products, arithmetic and copies ran while one was open for 0% of the time, Pallas kernels for 0%

profile of v1, /device:TPU:1, one launch (start us, length us, event | category | flops | bytes accessed | tf_op | source)
XLA Modules:
  0.0 647.1 jit_solution(7749764605199366862)
XLA Ops:
  7.2 0.0 copy-start
  7.2 0.0 all-gather.2.cloned.1.call-start
  7.2 1.4 multiply_convert_fusion.1
  8.6 0.0 all-gather.2.cloned.1.call-update
  8.7 0.0 copy-start.3
  8.7 0.0 reduce-scatter.4.cloned.1.call-start
  8.7 0.0 copy-start.2
  8.7 1.2 copy.14
  10.0 0.0 copy-done.3
  10.0 0.0 copy-done.2
  10.0 0.2 multiply_convert_fusion
  10.2 15.2 %all_to_all.19 = bf16[128,8,128]{0,2,1:T(8,128)(2,1)S(1)} all-to-all(bf16[128,8,128]{0,2,1:T(8,128)(2,1)S(1)} %bitcast.13), channel_id=1, replica_groups=mesh['grp'=64,'rep'=8] {'rep'}, dimensions={1} | all-to-all | bytes 524288 | tf_op jit(solution)/shard_map/all_to_all | solution.py:12
  25.4 0.2 copy.15
  25.6 112.0 %all-gather.2.cloned.1.call-done = bf16[1024,512]{1,0:T(8,128)(2,1)} async-done(((bf16[16,512]{1,0:T(8,128)(2,1)}), bf16[1024,512]{1,0:T(8,128)(2,1)}) %all-gather.2.cloned.1.call-update) | async-done | bytes 1048592 | tf_op jit(solution)/shard_map/all_gather | solution.py:13
  137.6 0.0 copy-start.1
  137.6 1.6 fusion.5
  139.2 0.0 copy-done.1
  139.2 0.3 fusion.2
  139.5 0.3 fusion
  139.8 1.3 copy.17
  141.1 0.0 reduce-scatter.4.cloned.1.call-update
  141.2 0.0 all-reduce.2.cloned.1.call-start
  141.2 82.9 %reduce-scatter.4.cloned.1.call-done = f32[64,512]{1,0:T(8,128)} async-done(((f32[512,512]{1,0:T(8,128)}), f32[64,512]{1,0:T(8,128)}) %reduce-scatter.4.cloned.1.call-update) | async-done | bytes 131088
  224.1 1.7 copy.18
  225.8 0.0 all-reduce.2.cloned.1.call-update
  225.9 0.0 copy-done
  225.9 1.0 convolution_convert_fusion
  226.8 412.0 %all-reduce.2.cloned.1.call-done = f32[64,512]{0,1:T(8,128)} async-done(((f32[64,512]{0,1:T(8,128)}), f32[64,512]{0,1:T(8,128)}) %all-reduce.2.cloned.1.call-update) | async-done | bytes 131088 | tf_op jit(solution)/shard_map/psum | solution.py:26
  638.8 1.0 broadcast_multiply_fusion
  639.8 0.8 copy.16
  (2 shorter events, 0.0 us)
Async XLA Ops:
  7.2 218.7 %copy-start = (bf16[512,512]{1,0:T(8,128)(2,1)S(1)}, bf16[512,512]{1,0:T(8,128)(2,1)}, u32[]{:S(2)}) copy-start(bf16[512,512]{1,0:T(8,128)(2,1)} %param.13) | copy-start | bytes 1572868
  7.2 130.4 %all-gather.2.cloned.1.call-start = ((), (), s32[]{:S(2)}) async-start(), calls=%async_computation.2 | async-start | bytes 1064960 | tf_op jit(solution)/shard_map/all_gather | solution.py:13
  8.7 1.3 copy-start.3
  8.7 215.4 %reduce-scatter.4.cloned.1.call-start = ((), (), s32[]{:S(2)}) async-start(), calls=%async_computation.4 | async-start | bytes 1179648
  8.7 1.3 copy-start.2
  137.6 1.6 copy-start.1
  141.2 497.6 %all-reduce.2.cloned.1.call-start = ((), (), s32[]{:S(2)}) async-start(), calls=%async_computation.3 | async-start | bytes 524288 | tf_op jit(solution)/shard_map/psum | solution.py:26
Sparse Core Ops, SparseCore 0:
  10.7 126.8 all-gather.1
  142.0 82.0 reduce-scatter.3
  227.0 411.7 all-reduce.1

commit v2 on v1

v2 whole, which is shorter than its diff:
```python
import jax
import jax.numpy as jnp
from jax import lax
from jax.experimental import pallas as pl
from jax.experimental.pallas import tpu as pltpu
from jax.sharding import PartitionSpec as P

MESH = pl.DeviceIdType.MESH
F32, BF16 = jnp.float32, jnp.bfloat16


def kernel(
    adjoint, active, counts, src_degree, dst_degree, inputs, weight,
    grad_input, grad_weight,
    masked, packed, tiles, inputs_t, half_out, half_in, own_half, plane_out, plane_in,
    ring_out, ring_in, total,
    tile_s, tile_r, mz_s, mz_r, my_s, my_r, mx_s, mx_r, mc_s, mc_r,
    half_s, half_r, plane_s, plane_r, ring_s, ring_r, tot_s, tot_r, last_s, last_r,
):
    grp, rep = lax.axis_index("grp"), lax.axis_index("rep")
    depth = masked.shape[0]
    z, quarter = lax.div(grp, 4), lax.rem(grp, 4)
    x_lo, core = lax.div(quarter, 2), lax.rem(quarter, 2)
    y, x_hi = lax.div(rep, 2), lax.rem(rep, 2)
    x = 2 * x_hi + x_lo

    def at_z(step):
        other = lax.rem(z + step, depth)
        return other, (other * 4 + quarter, rep)

    def at_plane(step):
        other_x, other_y = lax.rem(x + lax.div(step, 4), 4), lax.rem(y + lax.rem(step, 4), 4)
        other_lo = lax.rem(other_x, 2)
        other_rep = 2 * other_y + lax.div(other_x, 2)
        return other_lo, other_rep, (z * 4 + other_lo * 2 + core, other_rep)

    def at_rep(step):
        other = lax.rem(rep + step, 8)
        return other, (grp, other)

    def at_quarter(step):
        return (z * 4 + lax.rem(quarter + step, 4), rep)

    pair = (z * 4 + 2 * x_lo + 1 - core, rep)

    def copy(src, dst, send, recv, device):
        return pltpu.make_async_remote_copy(
            src_ref=src, dst_ref=dst, send_sem=send, recv_sem=recv,
            device_id=device, device_id_type=MESH,
        )

    def each(count, act):
        def turn(step, carry):
            act(step)
            return carry
        lax.fori_loop(1, count, turn, 0)

    barrier = pltpu.get_barrier_semaphore()

    def greet(device):
        pl.semaphore_signal(barrier, inc=1, device_id=device, device_id_type=MESH)

    each(16, lambda step: greet(at_plane(step)[2]))
    each(depth, lambda step: greet(at_z(step)[1]))
    greet(pair)
    greet((z * 4 + 2 * (1 - x_lo) + 1 - core, rep))

    columns = pl.ds(pl.multiple_of(y * 128, 128), 128)
    own = adjoint[:, columns].astype(F32) * active[:, columns].astype(F32)
    masked[z, quarter, :, columns] = own.astype(BF16)
    src_scale = lax.rsqrt(src_degree[...].astype(F32))
    src_scale = jnp.transpose(jnp.broadcast_to(src_scale, (128, 128)))
    dst_scale = lax.rsqrt(dst_degree[...].astype(F32))
    for part in range(8):
        cols = slice(128 * part, 128 * part + 128)
        scaled = counts[:, cols].astype(F32) * src_scale * dst_scale[:, cols]
        packed[part] = scaled.astype(BF16)
    tiles[rep] = packed[rep]
    inputs_t[...] = jnp.transpose(inputs[...])

    pl.semaphore_wait(barrier, 15 + depth - 1 + 2)

    def tile_copy(step):
        other, device = at_rep(step)
        return copy(packed.at[other], tiles.at[rep], tile_s.at[step], tile_r.at[step], device)

    def tile_wait(step):
        sender = lax.rem(rep + 8 - step, 8)
        copy(packed.at[0], tiles.at[sender], tile_s.at[step], tile_r.at[step], at_rep(step)[1]).wait_recv()

    def mz_copy(step):
        piece = masked.at[z, quarter, :, columns]
        return copy(piece, piece, mz_s.at[step], mz_r.at[step], at_z(step)[1])

    def mz_wait(step):
        sender = lax.rem(z + depth - step, depth)
        piece = masked.at[sender, quarter, :, columns]
        copy(piece, piece, mz_s.at[step], mz_r.at[step], at_z(step)[1]).wait_recv()

    def my_copy(step):
        piece = masked.at[:, quarter, :, columns]
        return copy(piece, piece, my_s.at[step], my_r.at[step], at_plane(step)[2])

    def my_wait(step):
        sender = lax.rem(y + 4 - step, 4)
        piece = masked.at[:, quarter, :, pl.ds(pl.multiple_of(sender * 128, 128), 128)]
        copy(piece, piece, my_s.at[step], my_r.at[step], at_plane(step)[2]).wait_recv()

    other_quarter = 2 * (1 - x_lo) + core
    half = depth // 2

    def mx_copy(which, at):
        piece = masked.at[pl.ds(which * half, half), at]
        return copy(piece, piece, mx_s.at[which], mx_r.at[which], at_plane(4 if which == 0 else 12)[2])

    def mc_copy(which, at):
        piece = masked.at[:, at]
        return copy(piece, piece, mc_s.at[which], mc_r.at[which], pair)

    def half_copy(lo):
        return copy(half_out.at[lo], half_in.at[lo], half_s.at[lo], half_r.at[lo], pair)

    def plane_copy(step):
        other_lo, other_rep, device = at_plane(step)
        rows = pl.ds(pl.multiple_of(other_rep * 64, 64), 64)
        return copy(plane_out.at[other_lo, rows], plane_in.at[step], plane_s.at[step], plane_r.at[step], device)

    def ring_copy(step):
        other, device = at_z(step)
        return copy(ring_out.at[other], ring_in.at[step], ring_s.at[step], ring_r.at[step], device)

    def tot_copy(step):
        piece = total.at[quarter, z]
        return copy(piece, piece, tot_s.at[step], tot_r.at[step], at_z(step)[1])

    def tot_wait(step):
        piece = total.at[quarter, lax.rem(z + depth - step, depth)]
        copy(piece, piece, tot_s.at[step], tot_r.at[step], at_z(step)[1]).wait_recv()

    def last_copy(step):
        piece = total.at[quarter]
        return copy(piece, piece, last_s.at[step], last_r.at[step], at_quarter(step))

    def last_wait(step):
        piece = total.at[lax.rem(quarter + 4 - step, 4)]
        copy(piece, piece, last_s.at[step], last_r.at[step], at_quarter(step)).wait_recv()

    each(8, lambda step: tile_copy(step).start())
    each(depth, lambda step: mz_copy(step).start())
    each(8, tile_wait)

    def term(span):
        rows = tiles[pl.ds(2 * span, 2)].reshape(256, 128)
        return lax.dot_general(
            inputs_t[...], rows, (((1,), (1,)), ((), ())), preferred_element_type=F32
        )

    for lo in range(2):
        half_out[lo] = term(2 * lo + 1 - core).astype(BF16)
        half_copy(lo).start()
    for lo in range(2):
        own_half[lo] = term(2 * lo + core)
    for lo in range(2):
        half_copy(lo).wait_recv()
        plane_out[lo] = (own_half[lo] + half_in[lo].astype(F32)).astype(BF16)
    each(16, lambda step: plane_copy(step).start())

    each(depth, mz_wait)
    each(4, lambda step: my_copy(step).start())

    rows = pl.ds(pl.multiple_of(rep * 64, 64), 64)
    summed = own_half[x_lo, rows] + half_in[x_lo, rows].astype(F32)
    each(16, lambda step: plane_copy(step).wait_recv())
    for step in range(1, 16):
        summed += plane_in[step].astype(F32)
    for side in range(2):
        ring_out[pl.ds(8 * side, 8)] = summed[:, 128 * side:128 * side + 128].reshape(8, 8, 128)
    each(depth, lambda step: ring_copy(step).start())

    each(4, my_wait)
    mx_copy(0, quarter).start()
    mx_copy(1, quarter).start()
    mc_copy(0, quarter).start()

    piece = ring_out[z]
    each(depth, lambda step: ring_copy(step).wait_recv())
    for step in range(1, depth):
        piece += ring_in[step]
    total[quarter, z] = piece
    each(depth, lambda step: tot_copy(step).start())

    mx_copy(0, other_quarter).wait_recv()
    mx_copy(1, other_quarter).wait_recv()
    mc_copy(1, other_quarter).start()
    mc_copy(0, 2 * x_lo + 1 - core).wait_recv()
    mc_copy(1, 2 * (1 - x_lo) + 1 - core).wait_recv()

    grad = jnp.zeros((128, 512), F32)
    for part in range(8):
        grad += lax.dot_general(
            jnp.transpose(tiles[part]), masked[2 * part:2 * part + 2].reshape(128, 512),
            (((1,), (0,)), ((), ())), preferred_element_type=F32,
        )
    grad_input[...] = lax.dot_general(
        grad.astype(BF16), weight[...], (((1,), (1,)), ((), ())), preferred_element_type=F32
    ).astype(BF16)

    each(depth, tot_wait)
    each(4, lambda step: last_copy(step).start())
    each(4, last_wait)
    out = jnp.zeros((64, 512), F32)
    for part in range(8):
        block = total[part // 2, 8 * (part % 2):8 * (part % 2) + 8].reshape(64, 128)
        high = block.astype(BF16)
        low = (block - high.astype(F32)).astype(BF16)
        both = lax.dot_general(
            jnp.concatenate([high, low], axis=0), masked[2 * part:2 * part + 2].reshape(128, 512),
            (((1,), (0,)), ((), ())), preferred_element_type=F32,
        )
        out += both[:64] + both[64:]
    grad_weight[...] = out * (1.0 / 65536.0)

    each(8, lambda step: tile_copy(step).wait_send())
    each(depth, lambda step: mz_copy(step).wait_send())
    each(4, lambda step: my_copy(step).wait_send())
    for which in range(2):
        mx_copy(which, quarter).wait_send()
        mc_copy(which, quarter).wait_send()
        half_copy(which).wait_send()
    each(16, lambda step: plane_copy(step).wait_send())
    each(depth, lambda step: ring_copy(step).wait_send())
    each(depth, lambda step: tot_copy(step).wait_send())
    each(4, lambda step: last_copy(step).wait_send())


def body(adjoint, active, counts, src_degree, dst_degree, inputs, weight):
    dma = pltpu.SemaphoreType.DMA
    vmem = pl.BlockSpec(memory_space=pltpu.VMEM)
    sems = []
    for count in (8, 16, 4, 2, 2, 2, 16, 16, 16, 4):
        sems += [dma((count,)), dma((count,))]
    return pl.pallas_call(
        kernel,
        out_shape=(
            jax.ShapeDtypeStruct((128, 512), BF16),
            jax.ShapeDtypeStruct((64, 512), F32),
        ),
        in_specs=[vmem] * 7,
        out_specs=(vmem, vmem),
        scratch_shapes=[
            pltpu.VMEM((16, 4, 16, 512), BF16),
            pltpu.VMEM((8, 128, 128), BF16),
            pltpu.VMEM((8, 128, 128), BF16),
            pltpu.VMEM((512, 128), BF16),
            pltpu.VMEM((2, 512, 256), BF16),
            pltpu.VMEM((2, 512, 256), BF16),
            pltpu.VMEM((2, 512, 256), F32),
            pltpu.VMEM((2, 512, 256), BF16),
            pltpu.VMEM((16, 64, 256), BF16),
            pltpu.VMEM((16, 8, 128), F32),
            pltpu.VMEM((16, 8, 128), F32),
            pltpu.VMEM((4, 16, 8, 128), F32),
        ] + sems,
        compiler_params=pltpu.CompilerParams(collective_id=0, has_side_effects=True),
    )(
        adjoint, active, counts, src_degree.reshape(1, 128), dst_degree.reshape(1, 1024),
        inputs, weight,
    )


def solution(mesh):
    in_specs = (
        P("grp", None),
        P("grp", None),
        P("rep", "grp"),
        P("rep"),
        P("grp"),
        P(("grp", "rep"), None),
        P(),
    )
    out_specs = (P(("grp", "rep"), None), P("rep", None))
    return jax.shard_map(body, mesh=mesh, in_specs=in_specs, out_specs=out_specs, check_vma=False)
```

time: 647 us -> 62.3 us (0.10)
  waiting for transfers between devices: 607 us -> 0 us
  Pallas kernels: 0 us -> 59.2 us
  blocking collectives: 15.2 us -> 0 us
  between operations: 13.9 us -> 0.65 us
    psum x1 -> x0, waiting for transfers between devices: 412 us -> none  [body(): grad_weight = lax.psum(part, 'grp')]
    all_gather x1 -> x0, waiting for transfers between devices: 112 us -> none  [body(): all_masked = lax.all_gather(masked, 'grp', axis=0, tiled=True)]
    unnamed x4 -> x0, waiting for transfers between devices: 82.9 us -> none
    pallas_call x0 -> x1, Pallas kernels: none -> 59.2 us  [body(): pl.pallas_call(kernel, out_shape=(jax.ShapeDtypeStruct((128, 512), BF16),...]
    all_to_all x1 -> x0, blocking collectives: 15.2 us -> none  [body(): lax.all_to_all(scaled, 'rep', split_axis=1, concat_axis=0, tiled=True)]
  transfers between devices with their start and end apart: 3 -> 0, of which waited for: 3 -> 0; matrix products, arithmetic and copies ran while one was open for 0% -> 0% of each run, Pallas kernels for 0% -> 0%
where the time goes in v2:
time: 62.3 us; the launch traced here: 62.2 us
  Pallas kernels  59.2 us (95%)
  local copies, waits for them, and re-layouts  2.26 us (4%)
  between operations  0.65 us (1%)
    pallas_call x1, Pallas kernels, body(): pl.pallas_call(kernel, out_shape=(jax.ShapeDtypeStruct((128, 512), BF16),...  59.2 us
    unnamed x4, local copies, waits for them, and re-layouts  2.26 us

profile of v2, /device:TPU:1, one launch (start us, length us, event | category | flops | bytes accessed | tf_op | source)
XLA Modules:
  0.0 62.2 jit_solution(8402824776124630006)
XLA Ops:
  0.6 59.2 %shard_map.86 = (bf16[128,512]{1,0:T(8,128)(2,1)}, f32[64,512]{1,0:T(8,128)}) custom-call(bf16[16,512]{1,0:T(8,128)(2,1)} %adjoint.1, s32[16,512]{1,0:T(8,128)} %active.1, s32[128,1024]{1,0:T(8,128)} %counts.1, s32[1,128]{1,0:T(1,128)} %bitcast.3, s32[1,1024]{1,0:T(1,128)} %bitcast.2, bf16[128,512]{1,0:T(8,128)(2,1)} %inputs.1, bf16[512,512]{1,0:T(8,128)(2,1)} %weight.1), custom_call_target="tpu_custom_call" | custom-call | tf_op jit(solution)/shard_map/pallas_call | solution.py:242
  59.9 0.0 copy-start
  59.9 1.6 %copy.11 = bf16[128,512]{1,0:T(8,128)(2,1)} copy(bf16[128,512]{1,0:T(8,128)(2,1)} %get-tuple-element.4) | data formatting | bytes 262144
  61.5 0.0 copy-done
  61.5 0.7 %copy.12 = f32[64,512]{1,0:T(8,128)} copy(f32[64,512]{1,0:T(8,128)S(1)} %copy-done) | data formatting | bytes 262144
Async XLA Ops:
  59.9 1.6 %copy-start = (f32[64,512]{1,0:T(8,128)S(1)}, f32[64,512]{1,0:T(8,128)}, u32[]{:S(2)}) copy-start(f32[64,512]{1,0:T(8,128)} %get-tuple-element.5) | copy-start | bytes 393220

commit v3 on v2

v3 whole, which is shorter than its diff:
```python
import jax
import jax.numpy as jnp
from jax import lax
from jax.experimental import pallas as pl
from jax.experimental.pallas import tpu as pltpu
from jax.sharding import PartitionSpec as P

MESH = pl.DeviceIdType.MESH
F32, BF16 = jnp.float32, jnp.bfloat16


def kernel(
    adjoint_h, active_h, counts_h, src_degree_h, dst_degree_h, inputs_h,
    high_h, sums_h,
    adjoint, active, counts, src_degree, dst_degree, inputs, high, sums,
    masked, packed, tiles, inputs_t, half_out, half_in, own_half, plane_out, plane_in,
    acc, ring_out, ring_in, total,
    load_s, save_s, token,
    tile_s, tile_r, mz_s, mz_r, my_s, my_r, mx_s, mx_r, mc_s, mc_r,
    half_s, half_r, plane_s, plane_r, ring_s, ring_r, tot_s, tot_r, cross_s, cross_r, last_s, last_r,
):
    grp, rep = lax.axis_index("grp"), lax.axis_index("rep")
    depth = masked.shape[0]
    z, quarter = lax.div(grp, 4), lax.rem(grp, 4)
    x_lo, core = lax.div(quarter, 2), lax.rem(quarter, 2)
    y, x_hi = lax.div(rep, 2), lax.rem(rep, 2)
    x = 2 * x_hi + x_lo
    across = 2 * (1 - x_lo) + core

    def at_z(step):
        other = lax.rem(z + step, depth)
        return other, (other * 4 + quarter, rep)

    def at_cross(step):
        return (lax.rem(z + step, depth) * 4 + across, rep)

    def at_plane(step):
        other_x, other_y = lax.rem(x + lax.div(step, 4), 4), lax.rem(y + lax.rem(step, 4), 4)
        other_lo = lax.rem(other_x, 2)
        other_rep = 2 * other_y + lax.div(other_x, 2)
        return other_lo, other_rep, (z * 4 + other_lo * 2 + core, other_rep)

    def at_rep(step):
        other = lax.rem(rep + step, 8)
        return other, (grp, other)

    pair = (z * 4 + 2 * x_lo + 1 - core, rep)

    def copy(src, dst, send, recv, device):
        return pltpu.make_async_remote_copy(
            src_ref=src, dst_ref=dst, send_sem=send, recv_sem=recv,
            device_id=device, device_id_type=MESH,
        )

    def each(low, count, act):
        def turn(step, carry):
            act(step)
            return carry
        lax.fori_loop(low, count, turn, 0)

    loads = [
        pltpu.make_async_copy(src, dst, load_s.at[index])
        for index, (src, dst) in enumerate((
            (counts_h, counts), (src_degree_h, src_degree), (dst_degree_h, dst_degree),
            (inputs_h, inputs), (adjoint_h, adjoint), (active_h, active),
        ))
    ]
    for load in loads:
        load.start()

    barrier = pltpu.get_barrier_semaphore()

    def greet(device):
        pl.semaphore_signal(barrier, inc=1, device_id=device, device_id_type=MESH)

    each(1, 16, lambda step: greet(at_plane(step)[2]))
    greet(pair)
    each(1, 5, lambda step: greet(at_z(step)[1]))
    each(depth - 4, depth, lambda step: greet(at_z(step)[1]))

    for load in loads[:3]:
        load.wait()
    src_scale = lax.rsqrt(src_degree[...].astype(F32))
    src_scale = jnp.transpose(jnp.broadcast_to(src_scale, (128, 128)))
    dst_scale = lax.rsqrt(dst_degree[...].astype(F32))
    for part in range(8):
        cols = slice(128 * part, 128 * part + 128)
        scaled = counts[:, cols].astype(F32) * src_scale * dst_scale[:, cols]
        packed[part] = scaled.astype(BF16)
    tiles[rep] = packed[rep]
    for load in loads[3:]:
        load.wait()
    turned = jnp.transpose(inputs[...])
    for part in range(8):
        for spot in range(4):
            at = 128 * (spot // 2) + 16 * part
            inputs_t[spot % 2, at:at + 16] = turned[64 * part + 16 * spot:64 * part + 16 * spot + 16]
    columns = pl.ds(pl.multiple_of(y * 128, 128), 128)
    own = adjoint[:, columns].astype(F32) * active[:, columns].astype(F32)
    masked[z, quarter, :, columns] = own.astype(BF16)

    pl.semaphore_wait(barrier, 15 + 1 + 8)

    def tile_copy(step):
        other, device = at_rep(step)
        return copy(packed.at[other], tiles.at[rep], tile_s.at[step], tile_r.at[step], device)

    def tile_wait(step):
        sender = lax.rem(rep + 8 - step, 8)
        copy(packed.at[0], tiles.at[sender], tile_s.at[step], tile_r.at[step], at_rep(step)[1]).wait_recv()

    def mz_copy(step):
        piece = masked.at[z, quarter, :, columns]
        return copy(piece, piece, mz_s.at[step], mz_r.at[step], at_z(step)[1])

    def mz_wait(step):
        piece = masked.at[lax.rem(z + depth - step, depth), quarter, :, columns]
        copy(piece, piece, mz_s.at[step], mz_r.at[step], at_z(step)[1]).wait_recv()

    def columns_of(which):
        return pl.ds(pl.multiple_of(which * 128, 128), 128)

    def my_copy(step):
        piece = masked.at[:, quarter, :, columns]
        return copy(piece, piece, my_s.at[step], my_r.at[step], at_plane(step)[2])

    def my_wait(step):
        piece = masked.at[:, quarter, :, columns_of(lax.rem(y + 4 - step, 4))]
        copy(piece, piece, my_s.at[step], my_r.at[step], at_plane(step)[2]).wait_recv()

    half = depth // 2

    def mx_copy(step):
        which, turn = lax.div(step, 4), lax.rem(step, 4)
        piece = masked.at[pl.ds(which * half, half), quarter, :, columns]
        return copy(piece, piece, mx_s.at[step], mx_r.at[step], at_plane(4 + 8 * which + turn)[2])

    def mx_wait(step):
        which, turn = lax.div(step, 4), lax.rem(step, 4)
        piece = masked.at[pl.ds(which * half, half), across, :, columns_of(lax.rem(y + 4 - turn, 4))]
        copy(piece, piece, mx_s.at[step], mx_r.at[step], at_plane(4 + 8 * which + turn)[2]).wait_recv()

    def mc_copy(which, at):
        piece = masked.at[:, at]
        return copy(piece, piece, mc_s.at[which], mc_r.at[which], pair)

    def half_copy(step):
        return copy(half_out.at[step], half_in.at[step], half_s.at[step], half_r.at[step], pair)

    def plane_copy(step, part, owner):
        other_lo, other_rep, device = at_plane(step)
        rows = pl.ds(pl.multiple_of((other_lo * 8 + other_rep) * 16, 16), 16)
        return copy(plane_out.at[part, rows], plane_in.at[step, owner], plane_s.at[step], plane_r.at[step], device)

    def plane_all(step):
        return copy(plane_in.at[step], plane_in.at[step], plane_s.at[step], plane_r.at[step], at_plane(step)[2])

    def ring_copy(step):
        other, device = at_z(step)
        return copy(ring_out.at[other], ring_in.at[step], ring_s.at[step], ring_r.at[step], device)

    def tot_copy(step):
        piece = total.at[quarter, z]
        return copy(piece, piece, tot_s.at[step], tot_r.at[step], at_z(step)[1])

    def tot_wait(step):
        piece = total.at[quarter, lax.rem(z + depth - step, depth)]
        copy(piece, piece, tot_s.at[step], tot_r.at[step], at_z(step)[1]).wait_recv()

    def cross_copy(step):
        piece = total.at[quarter, z]
        return copy(piece, piece, cross_s.at[step], cross_r.at[step], at_cross(step))

    def cross_wait(step):
        piece = total.at[across, lax.rem(z + depth - step, depth)]
        copy(piece, piece, cross_s.at[step], cross_r.at[step], at_cross(step)).wait_recv()

    def last_copy(which, at):
        piece = total.at[at]
        return copy(piece, piece, last_s.at[which], last_r.at[which], pair)

    each(1, 8, lambda step: tile_copy(step).start())
    for step in (4, depth - 4):
        pl.semaphore_signal(token, inc=1, device_id=at_z(step)[1], device_id_type=MESH)

    mine = pl.ds(pl.multiple_of((x_lo * 8 + rep) * 16, 16), 16)

    def term(side, owner):
        return lax.dot_general(
            inputs_t[side], tiles[owner], (((1,), (1,)), ((), ())), preferred_element_type=F32
        )

    def settle(step):
        owner = lax.rem(rep + 8 - step, 8)
        half_copy(step).wait_recv()
        plane_out[step] = (own_half[step] + half_in[step].astype(F32)).astype(BF16)
        each(1, 16, lambda other: plane_copy(other, step, owner).start())
        acc[pl.ds(pl.multiple_of(owner * 16, 16), 16)] = (
            own_half[step, mine] + half_in[step, mine].astype(F32)
        )

    for step in range(8):
        if step > 0:
            tile_wait(step)
        owner = lax.rem(rep + 8 - step, 8)
        half_out[step] = term(1 - core, owner).astype(BF16)
        half_copy(step).start()
        own_half[step] = term(core, owner)
        if step > 0:
            settle(step - 1)
        if step == 1:
            pl.semaphore_wait(token, 2)
            each(1, depth, lambda other: mz_copy(other).start())
    settle(7)

    each(1, depth, mz_wait)
    each(1, 4, lambda step: my_copy(step).start())
    each(0, 8, lambda step: mx_copy(step).start())

    summed = acc[...].reshape(8, 16, 128)
    each(1, 16, lambda step: plane_all(step).wait_recv())
    for step in range(1, 16):
        summed += plane_in[step].astype(F32)
    acc[...] = summed.reshape(128, 128)
    for row in range(depth):
        ring_out[row] = acc[pl.ds(row, 8, stride=16), :]
    each(1, depth, lambda step: ring_copy(step).start())

    each(1, 4, my_wait)
    mc_copy(0, quarter).start()
    each(0, 8, mx_wait)
    mc_copy(1, across).start()
    mc_copy(0, 2 * x_lo + 1 - core).wait_recv()
    mc_copy(1, 2 * (1 - x_lo) + 1 - core).wait_recv()

    piece = ring_out[z]
    each(1, depth, lambda step: ring_copy(step).wait_recv())
    for step in range(1, depth):
        piece += ring_in[step]
    upper = piece.astype(BF16)
    lower = (piece - upper.astype(F32)).astype(BF16)
    both = jnp.concatenate([upper, lower], axis=0)
    which_row = lax.rem(lax.broadcasted_iota(jnp.int32, (16, 512), 0), 8)
    product = jnp.zeros((16, 512), F32)
    for part in range(8):
        block = lax.dot_general(
            both, masked[2 * part:2 * part + 2].reshape(128, 512),
            (((1,), (0,)), ((), ())), preferred_element_type=F32,
        )
        product += jnp.where(which_row == part, block, 0.0)
    total[quarter, z] = jnp.sum(product, axis=0, keepdims=True)
    each(0, depth, lambda step: cross_copy(step).start())
    each(1, depth, lambda step: tot_copy(step).start())

    grad = jnp.zeros((128, 512), F32)
    for part in range(8):
        grad += lax.dot_general(
            jnp.transpose(tiles[part]), masked[2 * part:2 * part + 2].reshape(128, 512),
            (((1,), (0,)), ((), ())), preferred_element_type=F32,
        )
    high[...] = grad.astype(BF16)
    save_high = pltpu.make_async_copy(high, high_h, save_s.at[0])
    save_high.start()

    each(1, depth, tot_wait)
    last_copy(0, quarter).start()
    each(0, depth, cross_wait)
    last_copy(1, across).start()
    last_copy(0, 2 * x_lo + 1 - core).wait_recv()
    last_copy(1, 2 * (1 - x_lo) + 1 - core).wait_recv()
    for spot in range(4):
        for row in range(depth):
            at = 16 * spot + row
            sums[at:at + 1, :] = total[spot, row]
    save_sums = pltpu.make_async_copy(sums, sums_h, save_s.at[1])
    save_sums.start()

    each(1, 8, lambda step: tile_copy(step).wait_send())
    each(1, depth, lambda step: mz_copy(step).wait_send())
    each(1, 4, lambda step: my_copy(step).wait_send())
    each(0, 8, lambda step: mx_copy(step).wait_send())
    each(0, 8, lambda step: half_copy(step).wait_send())
    for which in range(2):
        mc_copy(which, quarter).wait_send()
        last_copy(which, quarter).wait_send()
    each(1, 16, lambda step: plane_all(step).wait_send())
    each(1, depth, lambda step: ring_copy(step).wait_send())
    each(1, depth, lambda step: tot_copy(step).wait_send())
    each(0, depth, lambda step: cross_copy(step).wait_send())
    save_high.wait()
    save_sums.wait()


def body(adjoint, active, counts, src_degree, dst_degree, inputs, weight):
    dma = pltpu.SemaphoreType.DMA
    anywhere = pl.BlockSpec(memory_space=pl.ANY)
    sems = [dma((6,)), dma((2,)), pltpu.SemaphoreType.REGULAR]
    for count in (8, 16, 4, 8, 2, 8, 16, 16, 16, 16, 2):
        sems += [dma((count,)), dma((count,))]
    I32 = jnp.int32
    high, sums = pl.pallas_call(
        kernel,
        out_shape=(
            jax.ShapeDtypeStruct((128, 512), BF16),
            jax.ShapeDtypeStruct((64, 512), F32),
        ),
        in_specs=[anywhere] * 6,
        out_specs=(anywhere, anywhere),
        scratch_shapes=[
            pltpu.VMEM(shape, kind) for shape, kind in (
                ((16, 512), BF16), ((16, 512), I32), ((128, 1024), I32), ((1, 128), I32),
                ((1, 1024), I32), ((128, 512), BF16), ((128, 512), BF16), ((64, 512), F32),
                ((16, 4, 16, 512), BF16),
                ((8, 128, 128), BF16),
                ((8, 128, 128), BF16),
                ((2, 256, 128), BF16),
                ((8, 256, 128), BF16),
                ((8, 256, 128), BF16),
                ((8, 256, 128), F32),
                ((8, 256, 128), BF16),
                ((16, 8, 16, 128), BF16),
                ((128, 128), F32),
                ((16, 8, 128), F32),
                ((16, 8, 128), F32),
                ((4, 16, 1, 512), F32),
            )
        ] + sems,
        compiler_params=pltpu.CompilerParams(collective_id=0, has_side_effects=True),
    )(
        adjoint, active, counts, src_degree.reshape(1, 128), dst_degree.reshape(1, 1024), inputs,
    )
    grad_input = lax.dot_general(
        high, weight, (((1,), (1,)), ((), ())), preferred_element_type=F32
    ).astype(BF16)
    return grad_input, sums * (1.0 / 65536.0)


def solution(mesh):
    in_specs = (
        P("grp", None),
        P("grp", None),
        P("rep", "grp"),
        P("rep"),
        P("grp"),
        P(("grp", "rep"), None),
        P(),
    )
    out_specs = (P(("grp", "rep"), None), P("rep", None))
    return jax.shard_map(body, mesh=mesh, in_specs=in_specs, out_specs=out_specs, check_vma=False)
```

time: 62.3 us -> 52.6 us (0.84)
  Pallas kernels: 59.2 us -> 49.2 us
  local copies, waits for them, and re-layouts: 2.26 us -> 0.01 us
  matrix products: 0 us -> 1.9 us
  other arithmetic: 0 us -> 0.67 us
    pallas_call x1, Pallas kernels: 59.2 us -> 49.2 us  [body(): pl.pallas_call(kernel, out_shape=(jax.ShapeDtypeStruct((128, 512), BF16),...]
    unnamed x4, local copies, waits for them, and re-layouts: 2.26 us -> 0.01 us
    dot_general x0 -> x1, matrix products: none -> 1.9 us  [body(): lax.dot_general(high, weight, (((1,), (1,)), ((), ())), preferred_element...]
    mul x0 -> x1, other arithmetic: none -> 0.67 us  [body(): return (grad_input, sums * (1.0 / 65536.0))]
where the time goes in v3:
time: 52.6 us; the launch traced here: 52.5 us
  Pallas kernels  49.2 us (94%)
  matrix products  1.9 us (4%)
  other arithmetic  0.67 us (1%)
  between operations  0.66 us (1%)
    pallas_call x1, Pallas kernels, body(): pl.pallas_call(kernel, out_shape=(jax.ShapeDtypeStruct((128, 512), BF16),...  49.2 us
    dot_general x1, matrix products, body(): lax.dot_general(high, weight, (((1,), (1,)), ((), ())), preferred_element...  1.9 us

profile of v3, /device:TPU:1, one launch (start us, length us, event | category | flops | bytes accessed | tf_op | source)
XLA Modules:
  0.0 52.5 jit_solution(16087929627952904673)
XLA Ops:
  0.6 0.0 copy-start
  0.6 49.2 %shard_map.86 = (bf16[128,512]{1,0:T(8,128)(2,1)}, f32[64,512]{1,0:T(8,128)}) custom-call(bf16[16,512]{1,0:T(8,128)(2,1)} %adjoint_h.1, s32[16,512]{1,0:T(8,128)} %active_h.1, s32[128,1024]{1,0:T(8,128)} %counts_h.1, s32[1,128]{1,0:T(1,128)} %bitcast.5, s32[1,1024]{1,0:T(1,128)} %bitcast.4, bf16[128,512]{1,0:T(8,128)(2,1)} %inputs_h.1), custom_call_target="tpu_custom_call" | custom-call | tf_op jit(solution)/shard_map/pallas_call | solution.py:301
  49.9 0.0 copy-done
  49.9 0.0 copy-start.1
  49.9 1.9 %convolution_convert_fusion = bf16[128,512]{1,0:T(8,128)(2,1)} fusion(bf16[128,512]{1,0:T(8,128)(2,1)} %get-tuple-element.4, bf16[512,512]{1,0:T(8,128)(2,1)S(1)} %copy-done), kind=kOutput, calls=%fused_computation | convolution fusion | flops 67174400 | bytes 786432 | tf_op jit(solution)/shard_map/dot_general | solution.py:332
  51.8 0.0 copy-done.1
  51.8 0.7 %broadcast_multiply_fusion = f32[64,512]{1,0:T(8,128)} fusion(f32[64,512]{1,0:T(8,128)S(1)} %copy-done.1), kind=kLoop, calls=%fused_computation.1 | loop fusion | flops 32768 | bytes 262144 | tf_op jit(solution)/shard_map/mul | solution.py:335
Async XLA Ops:
  0.6 49.2 %copy-start = (bf16[512,512]{1,0:T(8,128)(2,1)S(1)}, bf16[512,512]{1,0:T(8,128)(2,1)}, u32[]{:S(2)}) copy-start(bf16[512,512]{1,0:T(8,128)(2,1)} %param.13) | copy-start | bytes 1572868
  49.9 1.9 %copy-start.1 = (f32[64,512]{1,0:T(8,128)S(1)}, f32[64,512]{1,0:T(8,128)}, u32[]{:S(2)}) copy-start(f32[64,512]{1,0:T(8,128)} %get-tuple-element.5) | copy-start | bytes 393220

commit v4 on v3

v4 whole, which is shorter than its diff:
```python
import jax
import jax.numpy as jnp
from jax import lax
from jax.experimental import pallas as pl
from jax.experimental.pallas import tpu as pltpu
from jax.sharding import PartitionSpec as P

MESH = pl.DeviceIdType.MESH
F32, BF16 = jnp.float32, jnp.bfloat16


def ring_far(step, size):
    return min(step, size - step)


PLANE_FAR = sorted(range(1, 16), key=lambda step: -ring_far(step // 4, 4) - ring_far(step % 4, 4))
Z_FAR = sorted(range(1, 16), key=lambda step: -ring_far(step, 16))
REP_NEAR = sorted(range(8), key=lambda step: ring_far(step // 2, 4) + 2 * (step % 2))


def kernel(
    adjoint_h, active_h, counts_h, src_degree_h, dst_degree_h, inputs_h, weight_h,
    grad_input, sums,
    adjoint, active, counts, src_degree, dst_degree, inputs, weight,
    masked, packed, tiles, inputs_t, half_out, half_in, own_half, plane_out, plane_in,
    acc, ring_out, ring_in, total,
    load_s, token,
    tile_s, tile_r, mz_s, mz_r, my_s, my_r, mx_s, mx_r, mc_s, mc_r,
    half_s, half_r, plane_s, plane_r, ring_s, ring_r, tot_s, tot_r, cross_s, cross_r, last_s, last_r,
):
    grp, rep = lax.axis_index("grp"), lax.axis_index("rep")
    depth = masked.shape[0]
    z, quarter = lax.div(grp, 4), lax.rem(grp, 4)
    x_lo, core = lax.div(quarter, 2), lax.rem(quarter, 2)
    y, x_hi = lax.div(rep, 2), lax.rem(rep, 2)
    x = 2 * x_hi + x_lo
    across = 2 * (1 - x_lo) + core

    def at_z(step):
        other = lax.rem(z + step, depth)
        return other, (other * 4 + quarter, rep)

    def at_cross(step):
        return (lax.rem(z + step, depth) * 4 + across, rep)

    def at_plane(step):
        other_x, other_y = lax.rem(x + lax.div(step, 4), 4), lax.rem(y + lax.rem(step, 4), 4)
        other_lo = lax.rem(other_x, 2)
        other_rep = 2 * other_y + lax.div(other_x, 2)
        return other_lo, other_rep, (z * 4 + other_lo * 2 + core, other_rep)

    def rep_at(step, way):
        turn, flip = step // 2, step % 2
        return 2 * lax.rem(y + (turn if way > 0 else 4 - turn), 4) + lax.rem(x_hi + flip, 2)

    def at_rep(step):
        other = rep_at(step, 1)
        return other, (grp, other)

    pair = (z * 4 + 2 * x_lo + 1 - core, rep)

    def copy(src, dst, send, recv, device):
        return pltpu.make_async_remote_copy(
            src_ref=src, dst_ref=dst, send_sem=send, recv_sem=recv,
            device_id=device, device_id_type=MESH,
        )

    def each(low, count, act):
        def turn(step, carry):
            act(step)
            return carry
        lax.fori_loop(low, count, turn, 0)

    barrier = pltpu.get_barrier_semaphore()

    def greet(device):
        pl.semaphore_signal(barrier, inc=1, device_id=device, device_id_type=MESH)

    loads = [
        pltpu.make_async_copy(src, dst, load_s.at[index])
        for index, (src, dst) in enumerate((
            (counts_h, counts), (src_degree_h, src_degree), (dst_degree_h, dst_degree),
            (inputs_h, inputs), (adjoint_h, adjoint), (active_h, active),
            (weight_h, weight),
        ))
    ]
    for load in loads[:3]:
        load.start()
    planes = {step: at_plane(step) for step in range(1, 16)}
    for step in (4, 12):
        greet(at_z(step)[1])
    for step in PLANE_FAR:
        greet(planes[step][2])
    for step in (3, 13, 2, 14, 1, 15):
        greet(at_z(step)[1])
    greet(pair)
    for load in loads[3:]:
        load.start()

    for load in loads[:3]:
        load.wait()
    src_scale = lax.rsqrt(src_degree[...].astype(F32))
    src_scale = jnp.transpose(jnp.broadcast_to(src_scale, (128, 128)))
    dst_scale = lax.rsqrt(dst_degree[...].astype(F32))
    for part in range(8):
        cols = slice(128 * part, 128 * part + 128)
        scaled = counts[:, cols].astype(F32) * src_scale * dst_scale[:, cols]
        packed[part] = scaled.astype(BF16)
    tiles[rep] = packed[rep]
    pl.semaphore_wait(barrier, 15 + 1 + 8)

    def tile_copy(step):
        other, device = at_rep(step)
        return copy(packed.at[other], tiles.at[rep], tile_s.at[step], tile_r.at[step], device)

    def tile_wait(step):
        sender = rep_at(step, -1)
        copy(packed.at[0], tiles.at[sender], tile_s.at[step], tile_r.at[step], at_rep(step)[1]).wait_recv()

    def mz_copy(step):
        piece = masked.at[z, quarter, :, columns]
        return copy(piece, piece, mz_s.at[step], mz_r.at[step], at_z(step)[1])

    def mz_wait(step):
        piece = masked.at[lax.rem(z + depth - step, depth), quarter, :, columns]
        copy(piece, piece, mz_s.at[step], mz_r.at[step], at_z(step)[1]).wait_recv()

    def columns_of(which):
        return pl.ds(pl.multiple_of(which * 128, 128), 128)

    def my_copy(step):
        piece = masked.at[:, quarter, :, columns]
        return copy(piece, piece, my_s.at[step], my_r.at[step], at_plane(step)[2])

    def my_wait(step):
        piece = masked.at[:, quarter, :, columns_of(lax.rem(y + 4 - step, 4))]
        copy(piece, piece, my_s.at[step], my_r.at[step], at_plane(step)[2]).wait_recv()

    half = depth // 2

    def mx_copy(step):
        which, turn = lax.div(step, 4), lax.rem(step, 4)
        piece = masked.at[pl.ds(which * half, half), quarter, :, columns]
        return copy(piece, piece, mx_s.at[step], mx_r.at[step], at_plane(4 + 8 * which + turn)[2])

    def mx_wait(step):
        which, turn = lax.div(step, 4), lax.rem(step, 4)
        piece = masked.at[pl.ds(which * half, half), across, :, columns_of(lax.rem(y + 4 - turn, 4))]
        copy(piece, piece, mx_s.at[step], mx_r.at[step], at_plane(4 + 8 * which + turn)[2]).wait_recv()

    def mc_copy(which, at):
        piece = masked.at[:, at]
        return copy(piece, piece, mc_s.at[which], mc_r.at[which], pair)

    def half_copy(step):
        return copy(half_out.at[step], half_in.at[step], half_s.at[step], half_r.at[step], pair)

    def plane_copy(step, part, owner):
        other_lo, other_rep, device = planes[step]
        rows = pl.ds(pl.multiple_of((other_lo * 8 + other_rep) * 16, 16), 16)
        return copy(plane_out.at[part, rows], plane_in.at[step, owner], plane_s.at[step], plane_r.at[step], device)

    def plane_all(step):
        return copy(plane_in.at[step], plane_in.at[step], plane_s.at[step], plane_r.at[step], at_plane(step)[2])

    def ring_copy(step):
        other, device = at_z(step)
        return copy(ring_out.at[other], ring_in.at[step], ring_s.at[step], ring_r.at[step], device)

    def tot_copy(step):
        piece = total.at[quarter, z]
        return copy(piece, piece, tot_s.at[step], tot_r.at[step], at_z(step)[1])

    def tot_wait(step):
        piece = total.at[quarter, lax.rem(z + depth - step, depth)]
        copy(piece, piece, tot_s.at[step], tot_r.at[step], at_z(step)[1]).wait_recv()

    def cross_copy(step):
        piece = total.at[quarter, z]
        return copy(piece, piece, cross_s.at[step], cross_r.at[step], at_cross(step))

    def cross_wait(step):
        piece = total.at[across, lax.rem(z + depth - step, depth)]
        copy(piece, piece, cross_s.at[step], cross_r.at[step], at_cross(step)).wait_recv()

    def last_copy(which, at):
        piece = total.at[at]
        return copy(piece, piece, last_s.at[which], last_r.at[which], pair)

    for step in reversed(REP_NEAR[1:]):
        tile_copy(step).start()
    for step in (4, depth - 4):
        pl.semaphore_signal(token, inc=1, device_id=at_z(step)[1], device_id_type=MESH)

    for load in loads[3:6]:
        load.wait()
    turned = jnp.transpose(inputs[...])
    for part in range(8):
        for spot in range(4):
            at = 128 * (spot // 2) + 16 * part
            inputs_t[spot % 2, at:at + 16] = turned[64 * part + 16 * spot:64 * part + 16 * spot + 16]
    columns = pl.ds(pl.multiple_of(y * 128, 128), 128)
    own = adjoint[:, columns].astype(F32) * active[:, columns].astype(F32)
    masked[z, quarter, :, columns] = own.astype(BF16)

    mine = pl.ds(pl.multiple_of((x_lo * 8 + rep) * 16, 16), 16)

    def term(side, owner):
        return lax.dot_general(
            inputs_t[side], tiles[owner], (((1,), (1,)), ((), ())), preferred_element_type=F32
        )

    def settle(step):
        owner = rep_at(REP_NEAR[step], -1)
        half_copy(step).wait_recv()
        plane_out[step] = (own_half[step] + half_in[step].astype(F32)).astype(BF16)
        for other in PLANE_FAR:
            plane_copy(other, step, owner).start()
        acc[pl.ds(pl.multiple_of(owner * 16, 16), 16)] = (
            own_half[step, mine] + half_in[step, mine].astype(F32)
        )

    for step in range(8):
        if step > 0:
            tile_wait(REP_NEAR[step])
        owner = rep_at(REP_NEAR[step], -1)
        half_out[step] = term(1 - core, owner).astype(BF16)
        half_copy(step).start()
        own_half[step] = term(core, owner)
        if step > 0:
            settle(step - 1)
        if step == 1:
            pl.semaphore_wait(token, 2)
            for other in Z_FAR:
                mz_copy(other).start()
    settle(7)

    each(1, depth, mz_wait)
    each(1, 4, lambda step: my_copy(step).start())
    each(0, 8, lambda step: mx_copy(step).start())

    summed = acc[...].reshape(8, 16, 128)
    for step in reversed(PLANE_FAR):
        plane_all(step).wait_recv()
        summed += plane_in[step].astype(F32)
    acc[...] = summed.reshape(128, 128)
    for row in range(depth):
        ring_out[row] = acc[pl.ds(row, 8, stride=16), :]
    for step in Z_FAR:
        ring_copy(step).start()

    each(1, 4, my_wait)
    mc_copy(0, quarter).start()
    each(0, 8, mx_wait)
    mc_copy(1, across).start()
    mc_copy(0, 2 * x_lo + 1 - core).wait_recv()
    mc_copy(1, 2 * (1 - x_lo) + 1 - core).wait_recv()

    piece = ring_out[z]
    for step in reversed(Z_FAR):
        ring_copy(step).wait_recv()
        piece += ring_in[step]
    upper = piece.astype(BF16)
    lower = (piece - upper.astype(F32)).astype(BF16)
    both = jnp.concatenate([upper, lower], axis=0)
    which_row = lax.rem(lax.broadcasted_iota(jnp.int32, (16, 512), 0), 8)
    product = jnp.zeros((16, 512), F32)
    for part in range(8):
        block = lax.dot_general(
            both, masked[2 * part:2 * part + 2].reshape(128, 512),
            (((1,), (0,)), ((), ())), preferred_element_type=F32,
        )
        product += jnp.where(which_row == part, block, 0.0)
    total[quarter, z] = jnp.sum(product, axis=0, keepdims=True) * (1.0 / 65536.0)
    for step in Z_FAR:
        cross_copy(step).start()
        tot_copy(step).start()
    cross_copy(0).start()

    grad = jnp.zeros((128, 512), F32)
    for part in range(8):
        grad += lax.dot_general(
            jnp.transpose(tiles[part]), masked[2 * part:2 * part + 2].reshape(128, 512),
            (((1,), (0,)), ((), ())), preferred_element_type=F32,
        )
    loads[6].wait()
    grad_input[...] = lax.dot_general(
        grad.astype(BF16), weight[...], (((1,), (1,)), ((), ())), preferred_element_type=F32
    ).astype(BF16)

    each(1, depth, tot_wait)
    last_copy(0, quarter).start()
    each(0, depth, cross_wait)
    last_copy(1, across).start()
    last_copy(0, 2 * x_lo + 1 - core).wait_recv()
    last_copy(1, 2 * (1 - x_lo) + 1 - core).wait_recv()
    for spot in range(4):
        for row in range(depth):
            at = 16 * spot + row
            sums[at:at + 1, :] = total[spot, row]

    each(1, 8, lambda step: tile_copy(step).wait_send())
    each(1, depth, lambda step: mz_copy(step).wait_send())
    each(1, 4, lambda step: my_copy(step).wait_send())
    each(0, 8, lambda step: mx_copy(step).wait_send())
    each(0, 8, lambda step: half_copy(step).wait_send())
    for which in range(2):
        mc_copy(which, quarter).wait_send()
        last_copy(which, quarter).wait_send()
    each(1, 16, lambda step: plane_all(step).wait_send())
    each(1, depth, lambda step: ring_copy(step).wait_send())
    each(1, depth, lambda step: tot_copy(step).wait_send())
    each(0, depth, lambda step: cross_copy(step).wait_send())


def store(near_input, near_weight, far_input, far_weight, done):
    copies = (
        pltpu.make_async_copy(near_input, far_input, done.at[0]),
        pltpu.make_async_copy(near_weight, far_weight, done.at[1]),
    )
    for copy in copies:
        copy.start()
    for copy in copies:
        copy.wait()


def body(adjoint, active, counts, src_degree, dst_degree, inputs, weight):
    dma = pltpu.SemaphoreType.DMA
    far, near = pl.BlockSpec(memory_space=pltpu.HBM), pl.BlockSpec(memory_space=pltpu.VMEM)
    sems = [dma((7,)), pltpu.SemaphoreType.REGULAR]
    for count in (8, 16, 4, 8, 2, 8, 16, 16, 16, 16, 2):
        sems += [dma((count,)), dma((count,))]
    I32 = jnp.int32
    results = (pltpu.VMEM((128, 512), BF16), pltpu.VMEM((64, 512), F32))
    grad_input, sums = pl.pallas_call(
        kernel,
        out_shape=results,
        in_specs=[far] * 7,
        out_specs=(near, near),
        scratch_shapes=[
            pltpu.VMEM(shape, kind) for shape, kind in (
                ((16, 512), BF16), ((16, 512), I32), ((128, 1024), I32), ((1, 128), I32),
                ((1, 1024), I32), ((128, 512), BF16), ((512, 512), BF16),
                ((16, 4, 16, 512), BF16),
                ((8, 128, 128), BF16),
                ((8, 128, 128), BF16),
                ((2, 256, 128), BF16),
                ((8, 256, 128), BF16),
                ((8, 256, 128), BF16),
                ((8, 256, 128), F32),
                ((8, 256, 128), BF16),
                ((16, 8, 16, 128), BF16),
                ((128, 128), F32),
                ((16, 8, 128), F32),
                ((16, 8, 128), F32),
                ((4, 16, 1, 512), F32),
            )
        ] + sems,
        compiler_params=pltpu.CompilerParams(
            collective_id=0, has_side_effects=True, vmem_limit_bytes=56 * 1024 * 1024
        ),
    )(
        adjoint, active, counts, src_degree.reshape(1, 128), dst_degree.reshape(1, 1024), inputs,
        weight,
    )
    return tuple(pl.pallas_call(
        store,
        out_shape=(
            jax.ShapeDtypeStruct((128, 512), BF16),
            jax.ShapeDtypeStruct((64, 512), F32),
        ),
        in_specs=[near, near],
        out_specs=(far, far),
        scratch_shapes=[dma((2,))], compiler_params=pltpu.CompilerParams(vmem_limit_bytes=1024 * 1024),
    )(grad_input, sums))


def solution(mesh):
    in_specs = (
        P("grp", None),
        P("grp", None),
        P("rep", "grp"),
        P("rep"),
        P("grp"),
        P(("grp", "rep"), None),
        P(),
    )
    out_specs = (P(("grp", "rep"), None), P("rep", None))
    return jax.shard_map(body, mesh=mesh, in_specs=in_specs, out_specs=out_specs, check_vma=False)
```

time: 52.6 us -> 49 us (0.932)
  matrix products: 1.9 us -> 0 us
  Pallas kernels: 49.2 us -> 48.3 us
  other arithmetic: 0.67 us -> 0 us
    dot_general x1 -> x0, matrix products: 1.9 us -> none  [body(): lax.dot_general(high, weight, (((1,), (1,)), ((), ())), preferred_element...]
    pallas_call x1 -> x2, Pallas kernels: 49.2 us -> 48.3 us  [the longest x1 47.5 us: body(): pl.pallas_call(kernel, out_shape=results, in_specs=[far] * 7, out_specs=(...]
    mul x1 -> x0, other arithmetic: 0.67 us -> none  [body(): return (grad_input, sums * (1.0 / 65536.0))]
where the time goes in v4:
time: 49 us; the launch traced here: 48.9 us
  Pallas kernels  48.3 us (99%)
  between operations  0.64 us (1%)
    pallas_call x1, Pallas kernels, body(): pl.pallas_call(kernel, out_shape=results, in_specs=[far] * 7, out_specs=(...  47.5 us

profile of v4, /device:TPU:1, one launch (start us, length us, event | category | flops | bytes accessed | tf_op | source)
XLA Modules:
  0.0 48.9 jit_solution(1244360250519425716)
XLA Ops:
  0.6 47.5 %shard_map.86 = (bf16[128,512]{1,0:T(8,128)(2,1)S(1)}, f32[64,512]{1,0:T(8,128)S(1)}) custom-call(bf16[16,512]{1,0:T(8,128)(2,1)} %adjoint_h.1, s32[16,512]{1,0:T(8,128)} %active_h.1, s32[128,1024]{1,0:T(8,128)} %counts_h.1, s32[1,128]{1,0:T(1,128)} %bitcast.3, s32[1,1024]{1,0:T(1,128)} %bitcast.2, bf16[128,512]{1,0:T(8,128)(2,1)} %inputs_h.1, ...), custom_call_target="tpu_custom_call" | custom-call | tf_op jit(solution)/shard_map/pallas_call | solution.py:335
  48.2 0.7 %shard_map.87 = (bf16[128,512]{1,0:T(8,128)(2,1)}, f32[64,512]{1,0:T(8,128)}) custom-call(bf16[128,512]{1,0:T(8,128)(2,1)S(1)} %get-tuple-element.4.near_input, f32[64,512]{1,0:T(8,128)S(1)} %get-tuple-element.5.near_weight), custom_call_target="tpu_custom_call" | custom-call | tf_op jit(solution)/shard_map/pallas_call | solution.py:366

commit v5 on v4

--- a/solution.py
+++ b/solution.py
@@ -111,81 +111,69 @@
 
     def tile_copy(step):
         other, device = at_rep(step)
-        return copy(packed.at[other], tiles.at[rep], tile_s.at[step], tile_r.at[step], device)
+        return copy(packed.at[other], tiles.at[rep], tile_s, tile_r.at[step], device)
 
     def tile_wait(step):
         sender = rep_at(step, -1)
-        copy(packed.at[0], tiles.at[sender], tile_s.at[step], tile_r.at[step], at_rep(step)[1]).wait_recv()
+        copy(packed.at[0], tiles.at[sender], tile_s, tile_r.at[step], at_rep(step)[1]).wait_recv()
 
     def mz_copy(step):
         piece = masked.at[z, quarter, :, columns]
-        return copy(piece, piece, mz_s.at[step], mz_r.at[step], at_z(step)[1])
-
-    def mz_wait(step):
-        piece = masked.at[lax.rem(z + depth - step, depth), quarter, :, columns]
-        copy(piece, piece, mz_s.at[step], mz_r.at[step], at_z(step)[1]).wait_recv()
-
-    def columns_of(which):
-        return pl.ds(pl.multiple_of(which * 128, 128), 128)
+        return copy(piece, piece, mz_s, mz_r, at_z(step)[1])
+
+    def whole(ref, send, recv):
+        return copy(ref, ref, send, recv, pair)
+
+    mz_all = whole(masked.at[pl.ds(0, depth - 1), 0, :, pl.ds(0, 128)], mz_s, mz_r)
+    my_all = whole(masked.at[pl.ds(0, depth), pl.ds(0, 3), :, pl.ds(0, 128)], my_s, my_r)
+    mx_all = whole(masked.at[pl.ds(0, depth), 0], mx_s, mx_r)
+    mc_sent = whole(masked.at[pl.ds(0, depth), pl.ds(0, 2)], mc_s, mc_r.at[0])
+    tile_sent = whole(packed.at[pl.ds(0, 7)], tile_s, tile_r.at[0])
+    half_sent = whole(half_out.at[pl.ds(0, 8)], half_s, half_r.at[0])
+    plane_all = whole(plane_in.at[pl.ds(1, 15)], plane_s, plane_r)
+    ring_all = whole(ring_in.at[pl.ds(1, depth - 1)], ring_s, ring_r)
+    tot_all = whole(total.at[0, pl.ds(0, depth - 1)], tot_s, tot_r)
+    cross_all = whole(total.at[0, pl.ds(0, depth)], cross_s, cross_r)
+    last_sent = whole(total.at[pl.ds(0, 2)], last_s, last_r.at[0])
 
     def my_copy(step):
         piece = masked.at[:, quarter, :, columns]
-        return copy(piece, piece, my_s.at[step], my_r.at[step], at_plane(step)[2])
-
-    def my_wait(step):
-        piece = masked.at[:, quarter, :, columns_of(lax.rem(y + 4 - step, 4))]
-        copy(piece, piece, my_s.at[step], my_r.at[step], at_plane(step)[2]).wait_recv()
+        return copy(piece, piece, my_s, my_r, at_plane(step)[2])
 
     half = depth // 2
 
     def mx_copy(step):
         which, turn = lax.div(step, 4), lax.rem(step, 4)
         piece = masked.at[pl.ds(which * half, half), quarter, :, columns]
-        return copy(piece, piece, mx_s.at[step], mx_r.at[step], at_plane(4 + 8 * which + turn)[2])
-
-    def mx_wait(step):
-        which, turn = lax.div(step, 4), lax.rem(step, 4)
-        piece = masked.at[pl.ds(which * half, half), across, :, columns_of(lax.rem(y + 4 - turn, 4))]
-        copy(piece, piece, mx_s.at[step], mx_r.at[step], at_plane(4 + 8 * which + turn)[2]).wait_recv()
+        return copy(piece, piece, mx_s, mx_r, at_plane(4 + 8 * which + turn)[2])
 
     def mc_copy(which, at):
         piece = masked.at[:, at]
-        return copy(piece, piece, mc_s.at[which], mc_r.at[which], pair)
+        return copy(piece, piece, mc_s, mc_r.at[which], pair)
 
     def half_copy(step):
-        return copy(half_out.at[step], half_in.at[step], half_s.at[step], half_r.at[step], pair)
+        return copy(half_out.at[step], half_in.at[step], half_s, half_r.at[step], pair)
 
     def plane_copy(step, part, owner):
         other_lo, other_rep, device = planes[step]
         rows = pl.ds(pl.multiple_of((other_lo * 8 + other_rep) * 16, 16), 16)
-        return copy(plane_out.at[part, rows], plane_in.at[step, owner], plane_s.at[step], plane_r.at[step], device)
-
-    def plane_all(step):
-        return copy(plane_in.at[step], plane_in.at[step], plane_s.at[step], plane_r.at[step], at_plane(step)[2])
+        return copy(plane_out.at[part, rows], plane_in.at[step, owner], plane_s, plane_r, device)
 
     def ring_copy(step):
         other, device = at_z(step)
-        return copy(ring_out.at[other], ring_in.at[step], ring_s.at[step], ring_r.at[step], device)
+        return copy(ring_out.at[other], ring_in.at[step], ring_s, ring_r, device)
 
     def tot_copy(step):
         piece = total.at[quarter, z]
-        return copy(piece, piece, tot_s.at[step], tot_r.at[step], at_z(step)[1])
-
-    def tot_wait(step):
-        piece = total.at[quarter, lax.rem(z + depth - step, depth)]
-        copy(piece, piece, tot_s.at[step], tot_r.at[step], at_z(step)[1]).wait_recv()
+        return copy(piece, piece, tot_s, tot_r, at_z(step)[1])
 
     def cross_copy(step):
         piece = total.at[quarter, z]
-        return copy(piece, piece, cross_s.at[step], cross_r.at[step], at_cross(step))
-
-    def cross_wait(step):
-        piece = total.at[across, lax.rem(z + depth - step, depth)]
-        copy(piece, piece, cross_s.at[step], cross_r.at[step], at_cross(step)).wait_recv()
+        return copy(piece, piece, cross_s, cross_r, at_cross(step))
 
     def last_copy(which, at):
         piece = total.at[at]
-        return copy(piece, piece, last_s.at[which], last_r.at[which], pair)
+        return copy(piece, piece, last_s, last_r.at[which], pair)
 
     for step in reversed(REP_NEAR[1:]):
         tile_copy(step).start()
@@ -235,13 +223,13 @@
                 mz_copy(other).start()
     settle(7)
 
-    each(1, depth, mz_wait)
+    mz_all.wait_recv()
     each(1, 4, lambda step: my_copy(step).start())
     each(0, 8, lambda step: mx_copy(step).start())
 
     summed = acc[...].reshape(8, 16, 128)
-    for step in reversed(PLANE_FAR):
-        plane_all(step).wait_recv()
+    plane_all.wait_recv()
+    for step in range(1, 16):
         summed += plane_in[step].astype(F32)
     acc[...] = summed.reshape(128, 128)
     for row in range(depth):
@@ -249,16 +237,16 @@
     for step in Z_FAR:
         ring_copy(step).start()
 
-    each(1, 4, my_wait)
+    my_all.wait_recv()
     mc_copy(0, quarter).start()
-    each(0, 8, mx_wait)
+    mx_all.wait_recv()
     mc_copy(1, across).start()
     mc_copy(0, 2 * x_lo + 1 - core).wait_recv()
     mc_copy(1, 2 * (1 - x_lo) + 1 - core).wait_recv()
 
     piece = ring_out[z]
-    for step in reversed(Z_FAR):
-        ring_copy(step).wait_recv()
+    ring_all.wait_recv()
+    for step in range(1, depth):
         piece += ring_in[step]
     upper = piece.astype(BF16)
     lower = (piece - upper.astype(F32)).astype(BF16)
@@ -288,29 +276,26 @@
         grad.astype(BF16), weight[...], (((1,), (1,)), ((), ())), preferred_element_type=F32
     ).astype(BF16)
 
-    each(1, depth, tot_wait)
+    for sent in (tile_sent, mz_all, my_all, mx_all, mc_sent, half_sent, plane_all, ring_all):
+        sent.wait_send()
+
+    def place(spot):
+        for row in range(depth):
+            sums[pl.ds(spot * depth + row, 1), :] = total[spot, row]
+
+    tot_all.wait_recv()
     last_copy(0, quarter).start()
-    each(0, depth, cross_wait)
+    cross_all.wait_recv()
     last_copy(1, across).start()
+    place(quarter)
+    place(across)
+    tot_all.wait_send()
+    cross_all.wait_send()
     last_copy(0, 2 * x_lo + 1 - core).wait_recv()
+    place(2 * x_lo + 1 - core)
     last_copy(1, 2 * (1 - x_lo) + 1 - core).wait_recv()
-    for spot in range(4):
-        for row in range(depth):
-            at = 16 * spot + row
-            sums[at:at + 1, :] = total[spot, row]
-
-    each(1, 8, lambda step: tile_copy(step).wait_send())
-    each(1, depth, lambda step: mz_copy(step).wait_send())
-    each(1, 4, lambda step: my_copy(step).wait_send())
-    each(0, 8, lambda step: mx_copy(step).wait_send())
-    each(0, 8, lambda step: half_copy(step).wait_send())
-    for which in range(2):
-        mc_copy(which, quarter).wait_send()
-        last_copy(which, quarter).wait_send()
-    each(1, 16, lambda step: plane_all(step).wait_send())
-    each(1, depth, lambda step: ring_copy(step).wait_send())
-    each(1, depth, lambda step: tot_copy(step).wait_send())
-    each(0, depth, lambda step: cross_copy(step).wait_send())
+    place(2 * (1 - x_lo) + 1 - core)
+    last_sent.wait_send()
 
 
 def store(near_input, near_weight, far_input, far_weight, done):
@@ -328,8 +313,8 @@
     dma = pltpu.SemaphoreType.DMA
     far, near = pl.BlockSpec(memory_space=pltpu.HBM), pl.BlockSpec(memory_space=pltpu.VMEM)
     sems = [dma((7,)), pltpu.SemaphoreType.REGULAR]
-    for count in (8, 16, 4, 8, 2, 8, 16, 16, 16, 16, 2):
-        sems += [dma((count,)), dma((count,))]
+    for count in (8, 0, 0, 0, 2, 8, 0, 0, 0, 0, 2):
+        sems += [dma, dma((count,)) if count else dma]
     I32 = jnp.int32
     results = (pltpu.VMEM((128, 512), BF16), pltpu.VMEM((64, 512), F32))
     grad_input, sums = pl.pallas_call(

time: 49 us -> 46.7 us (0.953)
  Pallas kernels: 48.3 us -> 45.9 us
    pallas_call x1, Pallas kernels: 47.5 us -> 45.2 us  [body(): pl.pallas_call(kernel, out_shape=results, in_specs=[far] * 7, out_specs=(...]
where the time goes in v5:
time: 46.7 us; the launch traced here: 46.6 us
  Pallas kernels  45.9 us (98%)
  between operations  0.64 us (1%)
    pallas_call x1, Pallas kernels, body(): pl.pallas_call(kernel, out_shape=results, in_specs=[far] * 7, out_specs=(...  45.2 us

profile of v5, /device:TPU:1, one launch (start us, length us, event | category | flops | bytes accessed | tf_op | source)
XLA Modules:
  0.0 46.6 jit_solution(3183175446196643021)
XLA Ops:
  0.6 45.2 %shard_map.86 = (bf16[128,512]{1,0:T(8,128)(2,1)S(1)}, f32[64,512]{1,0:T(8,128)S(1)}) custom-call(bf16[16,512]{1,0:T(8,128)(2,1)} %adjoint_h.1, s32[16,512]{1,0:T(8,128)} %active_h.1, s32[128,1024]{1,0:T(8,128)} %counts_h.1, s32[1,128]{1,0:T(1,128)} %bitcast.3, s32[1,1024]{1,0:T(1,128)} %bitcast.2, bf16[128,512]{1,0:T(8,128)(2,1)} %inputs_h.1, ...), custom_call_target="tpu_custom_call" | custom-call | tf_op jit(solution)/shard_map/pallas_call | solution.py:320
  45.9 0.7 %shard_map.87 = (bf16[128,512]{1,0:T(8,128)(2,1)}, f32[64,512]{1,0:T(8,128)}) custom-call(bf16[128,512]{1,0:T(8,128)(2,1)S(1)} %get-tuple-element.4.near_input, f32[64,512]{1,0:T(8,128)S(1)} %get-tuple-element.5.near_weight), custom_call_target="tpu_custom_call" | custom-call | tf_op jit(solution)/shard_map/pallas_call | solution.py:351

commit v6 on v5

--- a/solution.py
+++ b/solution.py
@@ -190,6 +190,8 @@
     columns = pl.ds(pl.multiple_of(y * 128, 128), 128)
     own = adjoint[:, columns].astype(F32) * active[:, columns].astype(F32)
     masked[z, quarter, :, columns] = own.astype(BF16)
+    for step in Z_FAR[7:]:
+        mz_copy(step).start()
 
     mine = pl.ds(pl.multiple_of((x_lo * 8 + rep) * 16, 16), 16)
 
@@ -219,7 +221,7 @@
             settle(step - 1)
         if step == 1:
             pl.semaphore_wait(token, 2)
-            for other in Z_FAR:
+            for other in Z_FAR[:7]:
                 mz_copy(other).start()
     settle(7)
 
@@ -233,7 +235,7 @@
         summed += plane_in[step].astype(F32)
     acc[...] = summed.reshape(128, 128)
     for row in range(depth):
-        ring_out[row] = acc[pl.ds(row, 8, stride=16), :]
+        ring_out[row] = acc[pl.ds(row, 8, stride=16), :].astype(BF16)
     for step in Z_FAR:
         ring_copy(step).start()
 
@@ -244,10 +246,10 @@
     mc_copy(0, 2 * x_lo + 1 - core).wait_recv()
     mc_copy(1, 2 * (1 - x_lo) + 1 - core).wait_recv()
 
-    piece = ring_out[z]
+    piece = acc[pl.ds(z, 8, stride=16), :]
     ring_all.wait_recv()
     for step in range(1, depth):
-        piece += ring_in[step]
+        piece += ring_in[step].astype(F32)
     upper = piece.astype(BF16)
     lower = (piece - upper.astype(F32)).astype(BF16)
     both = jnp.concatenate([upper, lower], axis=0)
@@ -336,8 +338,8 @@
                 ((8, 256, 128), BF16),
                 ((16, 8, 16, 128), BF16),
                 ((128, 128), F32),
-                ((16, 8, 128), F32),
-                ((16, 8, 128), F32),
+                ((16, 8, 128), BF16),
+                ((16, 8, 128), BF16),
                 ((4, 16, 1, 512), F32),
             )
         ] + sems,

time: 46.7 us -> 46.6 us (level)
  no operation moved by 1% of the time
where the time goes in v6:
time: 46.6 us; the launch traced here: 46.5 us
  Pallas kernels  45.9 us (98%)
  between operations  0.64 us (1%)
    pallas_call x1, Pallas kernels, body(): pl.pallas_call(kernel, out_shape=results, in_specs=[far] * 7, out_specs=(...  45.1 us

profile of v6, /device:TPU:1, one launch (start us, length us, event | category | flops | bytes accessed | tf_op | source)
XLA Modules:
  0.0 46.5 jit_solution(4905671055611910335)
XLA Ops:
  0.6 45.1 %shard_map.86 = (bf16[128,512]{1,0:T(8,128)(2,1)S(1)}, f32[64,512]{1,0:T(8,128)S(1)}) custom-call(bf16[16,512]{1,0:T(8,128)(2,1)} %adjoint_h.1, s32[16,512]{1,0:T(8,128)} %active_h.1, s32[128,1024]{1,0:T(8,128)} %counts_h.1, s32[1,128]{1,0:T(1,128)} %bitcast.3, s32[1,1024]{1,0:T(1,128)} %bitcast.2, bf16[128,512]{1,0:T(8,128)(2,1)} %inputs_h.1, ...), custom_call_target="tpu_custom_call" | custom-call | tf_op jit(solution)/shard_map/pallas_call | solution.py:322
  45.8 0.7 %shard_map.87 = (bf16[128,512]{1,0:T(8,128)(2,1)}, f32[64,512]{1,0:T(8,128)}) custom-call(bf16[128,512]{1,0:T(8,128)(2,1)S(1)} %get-tuple-element.4.near_input, f32[64,512]{1,0:T(8,128)S(1)} %get-tuple-element.5.near_weight), custom_call_target="tpu_custom_call" | custom-call | tf_op jit(solution)/shard_map/pallas_call | solution.py:353

commit v7 on v5

--- a/solution.py
+++ b/solution.py
@@ -190,6 +190,8 @@
     columns = pl.ds(pl.multiple_of(y * 128, 128), 128)
     own = adjoint[:, columns].astype(F32) * active[:, columns].astype(F32)
     masked[z, quarter, :, columns] = own.astype(BF16)
+    for step in Z_FAR[7:]:
+        mz_copy(step).start()
 
     mine = pl.ds(pl.multiple_of((x_lo * 8 + rep) * 16, 16), 16)
 
@@ -219,7 +221,7 @@
             settle(step - 1)
         if step == 1:
             pl.semaphore_wait(token, 2)
-            for other in Z_FAR:
+            for other in Z_FAR[:7]:
                 mz_copy(other).start()
     settle(7)
 

time: 46.7 us -> 46.8 us (level)
  no operation moved by 1% of the time
where the time goes in v7:
time: 46.8 us; the launch traced here: 46.7 us
  Pallas kernels  46 us (98%)
  between operations  0.64 us (1%)
    pallas_call x1, Pallas kernels, body(): pl.pallas_call(kernel, out_shape=results, in_specs=[far] * 7, out_specs=(...  45.3 us

profile of v7, /device:TPU:1, one launch (start us, length us, event | category | flops | bytes accessed | tf_op | source)
XLA Modules:
  0.0 46.7 jit_solution(17341654564694718978)
XLA Ops:
  0.6 45.3 %shard_map.86 = (bf16[128,512]{1,0:T(8,128)(2,1)S(1)}, f32[64,512]{1,0:T(8,128)S(1)}) custom-call(bf16[16,512]{1,0:T(8,128)(2,1)} %adjoint_h.1, s32[16,512]{1,0:T(8,128)} %active_h.1, s32[128,1024]{1,0:T(8,128)} %counts_h.1, s32[1,128]{1,0:T(1,128)} %bitcast.3, s32[1,1024]{1,0:T(1,128)} %bitcast.2, bf16[128,512]{1,0:T(8,128)(2,1)} %inputs_h.1, ...), custom_call_target="tpu_custom_call" | custom-call | tf_op jit(solution)/shard_map/pallas_call | solution.py:322
  45.9 0.7 %shard_map.87 = (bf16[128,512]{1,0:T(8,128)(2,1)}, f32[64,512]{1,0:T(8,128)}) custom-call(bf16[128,512]{1,0:T(8,128)(2,1)S(1)} %get-tuple-element.4.near_input, f32[64,512]{1,0:T(8,128)S(1)} %get-tuple-element.5.near_weight), custom_call_target="tpu_custom_call" | custom-call | tf_op jit(solution)/shard_map/pallas_call | solution.py:353
